TPU v7x, 512 devices: a whole 4x4x16 slice. The times are simulated.
512 devices in a mesh: cluster: 64 (over y, z), member: 8 (over x, core).
Axes of the slice: x: 4, y: 4, z: 16, core: 2. Of those that a mesh axis runs over, the one named last changes fastest.
Arguments:
- leaf_centers: float32 [3, 512], replicated, may hold values from 0 to 1
- source_coords: float32 [3, 65536], P(None, ('cluster', 'member')), may hold values from -1 to 1
- target_points: float32 [3, 65536], P(None, ('cluster', 'member')), may hold values from 0 to 1
- charges: float32 [8, 65536], P(None, ('cluster', 'member')), may hold values from -6 to 6
- boundary_data: float32 [8, 65536], P(None, ('cluster', 'member')), may hold values from -6 to 6
- step_sizes: float32 [8], replicated, may hold values from 0.2 to 1
- valid_count: int32 [512], P(('cluster', 'member')), may hold values from 64 to 128, as said below
- near_lists: int32 [64, 26], replicated, may hold values from 0 to 63, as said below
Outputs:
- new_charges: float32 [8, 65536], P(None, ('cluster', 'member'))
- residual: float32 [8, 65536], P(None, ('cluster', 'member'))
Inputs may be any that keep to these rules, and one draw needn't show every extreme that they name: `valid_count`: some leaf has 128 live slots and some has half of 128. `near_lists`: row c names 26 different clusters, none of them c.
All inputs are finite; a program needn't handle non-finite values.
Results may differ from a plain program's by a relative error of at most 0.0003.
Values sent between devices are 32-bit elements; how exact they have to be, the bound alone decides.
No kernel may reach another device: no remote copies, remote signals or barrier semaphores. Data moves between devices by JAX's collectives and lax.ppermute only.
A program may use at most 64 MiB of HBM per device.

v0:
```python
import math
import jax
import jax.numpy as jnp
import numpy as np
from jax import lax
from jax.sharding import PartitionSpec as P

ITERS = 2
HALF_SIDE = 0.08
SOFTENING = 0.0025


def cheby_nodes(number):
    return np.cos(np.pi * (2 * np.arange(number) + 1) / (2 * number))


def basis_line(coord, number):
    nodes = cheby_nodes(number)
    factors = []
    for first in range(number):
        factor = jnp.ones_like(coord)
        for other in range(number):
            if other != first:
                factor = factor * (coord - nodes[other]) / (nodes[first] - nodes[other])
        factors.append(factor)
    return jnp.stack(factors, 0)


def lagrange(coords):
    along_x = basis_line(coords[0], 2)
    along_y = basis_line(coords[1], 4)
    along_z = basis_line(coords[2], 4)
    joined = along_x[:, None, None, :] * along_y[None, :, None, :] * along_z[None, None, :, :]
    return joined.reshape(32, coords.shape[1])


def proxy_grid():
    grid_x, grid_y, grid_z = np.meshgrid(
        cheby_nodes(2), cheby_nodes(4), cheby_nodes(4), indexing="ij"
    )
    return jnp.asarray(
        np.stack([grid_x.reshape(-1), grid_y.reshape(-1), grid_z.reshape(-1)], 0), jnp.float32
    )


def potential(targets, sources, weights):
    target_count = targets.shape[1]
    source_count = sources.shape[1]
    limit = max(128, (1 << 20) // target_count)
    src_block = math.gcd(source_count, limit)

    def advance(turn, running):
        pts = lax.dynamic_slice_in_dim(sources, turn * src_block, src_block, 1)
        wts = lax.dynamic_slice_in_dim(weights, turn * src_block, src_block, 1)
        distance = (pts[0][:, None] - targets[0][None, :]) ** 2
        distance = distance + (pts[1][:, None] - targets[1][None, :]) ** 2
        distance = distance + (pts[2][:, None] - targets[2][None, :]) ** 2
        kernel = lax.rsqrt(distance + SOFTENING)
        return running + jnp.dot(
            wts, kernel, precision=lax.Precision.HIGHEST, preferred_element_type=jnp.float32
        )

    start_value = jnp.zeros((weights.shape[0], target_count), jnp.float32)
    return lax.fori_loop(0, source_count // src_block, advance, start_value)


def flatten_packets(packets):
    return jnp.moveaxis(packets, 1, 0).reshape(packets.shape[1], -1)


def body(
    leaf_centers,
    source_coords,
    target_points,
    charges,
    boundary_data,
    step_sizes,
    valid_count,
    near_lists,
):
    clusters = lax.axis_size("cluster")
    members = lax.axis_size("member")
    leaf_size = source_coords.shape[1]
    proxies = 32
    cluster_index = lax.axis_index("cluster")
    member_index = lax.axis_index("member")
    leaf_index = cluster_index * members + member_index
    center = lax.dynamic_slice_in_dim(leaf_centers, leaf_index, 1, 1)
    source_points = center + HALF_SIDE * source_coords
    live = (jnp.arange(leaf_size, dtype=jnp.int32) < valid_count[0]).astype(jnp.float32)
    interp = lagrange(source_coords)
    offsets = proxy_grid()
    proxy_points = leaf_centers[:, :, None] + HALF_SIDE * offsets[:, None, :]
    my_near = lax.dynamic_index_in_dim(near_lists, cluster_index, 0, keepdims=False)
    listed = jnp.any(near_lists == cluster_index, axis=1)
    own_near = jnp.concatenate([jnp.reshape(cluster_index, (1,)), my_near])
    cluster_ids = jnp.arange(clusters, dtype=jnp.int32)
    far_cluster = jnp.all(cluster_ids[:, None] != own_near[None, :], axis=1).astype(jnp.float32)
    scale = 1.0 / math.sqrt(clusters * members * leaf_size)

    def outgoing(packet):
        return jnp.where(listed[:, None, None], packet[None], jnp.zeros_like(packet)[None])

    def select(received, own_piece):
        return jnp.concatenate([own_piece[None], jnp.take(received, my_near, axis=0)], 0)

    arrived_points = lax.all_to_all(
        outgoing(source_points), "cluster", split_axis=0, concat_axis=0, tiled=True
    )
    near_points = select(arrived_points, source_points)
    all_near_points = lax.all_gather(near_points, "member", axis=0, tiled=True)
    every_far = jnp.repeat(far_cluster, members * proxies)
    every_proxy = proxy_points.reshape(3, -1)
    current = charges * live
    residual = current
    for turn in range(ITERS):
        proxy_charges = jnp.einsum("fj,pj->fp", current, interp, precision=lax.Precision.HIGHEST)
        arrived_charges = lax.all_to_all(
            outgoing(current), "cluster", split_axis=0, concat_axis=0, tiled=True
        )
        near_charges = select(arrived_charges, current)
        near_sum = potential(
            target_points,
            flatten_packets(all_near_points),
            flatten_packets(lax.all_gather(near_charges, "member", axis=0, tiled=True)),
        )
        piece = lax.all_gather(proxy_charges, ("cluster", "member"), axis=1, tiled=True)
        positions = lax.slice_in_dim(every_proxy, 0, piece.shape[1], axis=1)
        far_sum = potential(target_points, positions, piece * every_far[None, :])
        field_sum = near_sum + far_sum
        residual = live * (boundary_data - scale * field_sum)
        current = live * (current + step_sizes[:, None] * residual / (1.0 + jnp.abs(residual)))
    return (current, residual)


def solution(mesh):
    in_specs = (
        P(),
        P(None, ("cluster", "member")),
        P(None, ("cluster", "member")),
        P(None, ("cluster", "member")),
        P(None, ("cluster", "member")),
        P(),
        P(("cluster", "member")),
        P(),
    )
    out_specs = (P(None, ("cluster", "member")), P(None, ("cluster", "member")))
    return jax.shard_map(body, mesh=mesh, in_specs=in_specs, out_specs=out_specs, check_vma=False)
```

profile of v0, /device:TPU:1, one launch (start us, length us, event | category | flops | bytes accessed | tf_op | source)
XLA Modules:
  0.0 408.0 jit_solution(5029262380854414042)
XLA Ops:
  1.4 0.9 dynamic-slice_reduce_fusion.1
  3.8 19.3 %all-to-all-start.1 = ((f32[64,3,128]{2,1,0:T(4,128)}), f32[64,3,128]{2,1,0:T(4,128)S(1)}, u32[]{:S(2)}, u32[]{:S(2)}) async-start(f32[64,3,128]{2,1,0:T(4,128)} %broadcast_select_fusion.2), calls=%async_computation.1 | async-start | bytes 262144 | tf_op jit(solution)/shard_map/all_to_all | solution.py:107
  23.1 0.9 dynamic-slice_reduce_fusion
  26.4 117.8 %all-gather = f32[512,32,8]{1,2,0:T(8,128)S(1)} all-gather(f32[1,32,8]{1,2,0:T(8,128)S(1)} %convolution_bitcast_fusion.1), channel_id=1, replica_groups=mesh['cluster'=64,'member'=8] {'cluster','member'}, dimensions={0}, use_global_device_ids=true | all-gather | bytes 525312 | tf_op jit(solution)/shard_map/all_gather | solution.py:127
  144.5 1.0 reshape.131
  146.6 10.0 %while.57 = (s32[]{:T(128)}, f32[8,128]{1,0:T(8,128)S(1)}, f32[8,16384]{1,0:T(8,128)S(1)}, f32[3,16384]{1,0:T(4,128)S(1)}, f32[3,128]{1,0:T(4,128)S(1)}, /*index...) while((s32[]{:T(128)}, f32[8,128]{1,0:T(8,128)S(1)}, ...), condition=%wide.region_5.7_spmd.clone, body=%wide.region_4.6_spmd.clone.sunk | while | flops 110102536 | bytes 570069 | solution.py:64
  146.9 4.8 %fusion.110 = f32[8,128]{1,0:T(8,128)S(1)} fusion(f32[128]{0:T(128)S(1)} %get-tuple-element.677, f32[8192]{0:T(1024)S(1)} %bitcast.113, f32[128]{0:T(128)S(1)} %get-tuple-element.679, f32[8192]{0:T(1024)S(1)} %bitcast.112, f32[128]{0:T(128)S(1)} %get-tuple-element.681, f32[8192]{0:T(1024)S(1)} %bitcast.111, f32[8,16384]{1,0:T(8,128)S(1)} %get-tuple-element.762, ...), kind=kOutput, calls=%fused_computation.46.clone.1 | convolution fusion | flops 110102528 | bytes 370181 | tf_op jit(solution)/shard_map/while/body/eval_jaxpr/dot_general | solution.py:59
  151.9 4.8 %fusion.110 = f32[8,128]{1,0:T(8,128)S(1)} fusion(f32[128]{0:T(128)S(1)} %get-tuple-element.677, f32[8192]{0:T(1024)S(1)} %bitcast.113, f32[128]{0:T(128)S(1)} %get-tuple-element.679, f32[8192]{0:T(1024)S(1)} %bitcast.112, f32[128]{0:T(128)S(1)} %get-tuple-element.681, f32[8192]{0:T(1024)S(1)} %bitcast.111, f32[8,16384]{1,0:T(8,128)S(1)} %get-tuple-element.762, ...), kind=kOutput, calls=%fused_computation.46.clone.1 | convolution fusion | flops 110102528 | bytes 370181 | tf_op jit(solution)/shard_map/while/body/eval_jaxpr/dot_general | solution.py:59
  156.7 0.8 broadcast_select_fusion.1
  157.6 11.6 %all-to-all-start = ((f32[64,8,128]{2,1,0:T(8,128)}), f32[64,8,128]{2,1,0:T(8,128)S(1)}, u32[]{:S(2)}, u32[]{:S(2)}) async-start(f32[64,8,128]{2,1,0:T(8,128)} %broadcast_select_fusion.1), calls=%async_computation | async-start | bytes 524288 | tf_op jit(solution)/shard_map/all_to_all | solution.py:118
  170.0 13.3 %all_gather.16 = f32[216,3,128]{2,1,0:T(4,128)S(1)} all-gather(f32[27,3,128]{2,1,0:T(4,128)S(1)} %pad_maximum_fusion.2), channel_id=1, replica_groups=mesh['cluster'=64,'member'=8] {'member'}, dimensions={0}, use_global_device_ids=true | all-gather | bytes 373248 | tf_op jit(solution)/shard_map/all_gather | solution.py:111
  183.3 5.9 %all-to-all-done = f32[64,8,128]{2,1,0:T(8,128)S(1)} async-done(((f32[64,8,128]{2,1,0:T(8,128)}), f32[64,8,128]{2,1,0:T(8,128)S(1)}, u32[]{:S(2)}, u32[]{:S(2)}) %all-to-all-start) | async-done | bytes 262176 | tf_op jit(solution)/shard_map/all_to_all | solution.py:118
  189.9 15.3 %all_gather.15 = f32[216,8,128]{2,1,0:T(8,128)S(1)} all-gather(f32[27,8,128]{2,1,0:T(8,128)S(1)} %pad_maximum_fusion), channel_id=1, replica_groups=mesh['cluster'=64,'member'=8] {'member'}, dimensions={0}, use_global_device_ids=true | all-gather | bytes 995328 | tf_op jit(solution)/shard_map/all_gather | solution.py:125
  205.2 23.9 %while.56 = (s32[]{:T(128)}, f32[8,128]{1,0:T(8,128)S(1)}, f32[8,27648]{1,0:T(8,128)S(1)}, f32[3,27648]{1,0:T(4,128)S(1)}, f32[3,128]{1,0:T(4,128)S(1)}, /*index...) while((s32[]{:T(128)}, f32[8,128]{1,0:T(8,128)S(1)}, ...), condition=%wide.region_2.4_spmd.clone, body=%wide.region_1.0_spmd.clone.sunk | while | flops 13764617 | bytes 82645 | solution.py:64
  229.1 0.8 broadcast_select_fusion
  230.1 7.5 %all-to-all-start.2 = ((f32[64,8,128]{2,1,0:T(8,128)}), f32[64,8,128]{2,1,0:T(8,128)}, u32[]{:S(2)}, u32[]{:S(2)}) async-start(f32[64,8,128]{2,1,0:T(8,128)} %broadcast_select_fusion), calls=%async_computation.2 | async-start | bytes 524288 | tf_op jit(solution)/shard_map/all_to_all | solution.py:118
  237.6 119.2 %all-gather.1 = f32[512,32,8]{1,2,0:T(8,128)S(1)} all-gather(f32[1,32,8]{1,2,0:T(8,128)S(1)} %convolution_bitcast_fusion), channel_id=1, replica_groups=mesh['cluster'=64,'member'=8] {'cluster','member'}, dimensions={0}, use_global_device_ids=true | all-gather | bytes 525312 | tf_op jit(solution)/shard_map/all_gather | solution.py:127
  357.2 1.0 reshape.133
  358.2 10.0 %while.59 = (s32[]{:T(128)}, f32[8,128]{1,0:T(8,128)S(1)}, f32[8,16384]{1,0:T(8,128)S(1)}, f32[3,16384]{1,0:T(4,128)S(1)}, f32[3,128]{1,0:T(4,128)S(1)}, /*index...) while((s32[]{:T(128)}, f32[8,128]{1,0:T(8,128)S(1)}, ...), condition=%wide.region_9.11_spmd.clone, body=%wide.region_8.10_spmd.clone.sunk | while | flops 110102536 | bytes 570069 | solution.py:64
  358.5 4.8 %fusion.115 = f32[8,128]{1,0:T(8,128)S(1)} fusion(f32[128]{0:T(128)S(1)} %get-tuple-element.699, f32[8192]{0:T(1024)S(1)} %bitcast.116, f32[128]{0:T(128)S(1)} %get-tuple-element.701, f32[8192]{0:T(1024)S(1)} %bitcast.115, f32[128]{0:T(128)S(1)} %get-tuple-element.703, f32[8192]{0:T(1024)S(1)} %bitcast.114, f32[8,16384]{1,0:T(8,128)S(1)} %get-tuple-element.828, ...), kind=kOutput, calls=%fused_computation.97.clone.1 | convolution fusion | flops 110102528 | bytes 370181 | tf_op jit(solution)/shard_map/while/body/eval_jaxpr/dot_general | solution.py:59
  363.5 4.8 %fusion.115 = f32[8,128]{1,0:T(8,128)S(1)} fusion(f32[128]{0:T(128)S(1)} %get-tuple-element.699, f32[8192]{0:T(1024)S(1)} %bitcast.116, f32[128]{0:T(128)S(1)} %get-tuple-element.701, f32[8192]{0:T(1024)S(1)} %bitcast.115, f32[128]{0:T(128)S(1)} %get-tuple-element.703, f32[8192]{0:T(1024)S(1)} %bitcast.114, f32[8,16384]{1,0:T(8,128)S(1)} %get-tuple-element.828, ...), kind=kOutput, calls=%fused_computation.97.clone.1 | convolution fusion | flops 110102528 | bytes 370181 | tf_op jit(solution)/shard_map/while/body/eval_jaxpr/dot_general | solution.py:59
  368.3 1.5 gather_fusion.2
  369.9 13.5 %all_gather.18 = f32[216,8,128]{2,1,0:T(8,128)S(1)} all-gather(f32[27,8,128]{2,1,0:T(8,128)S(1)} %pad_maximum_fusion.1), channel_id=1, replica_groups=mesh['cluster'=64,'member'=8] {'member'}, dimensions={0}, use_global_device_ids=true | all-gather | bytes 995328 | tf_op jit(solution)/shard_map/all_gather | solution.py:125
  383.4 23.9 %while.58 = (s32[]{:T(128)}, f32[8,128]{1,0:T(8,128)S(1)}, f32[8,27648]{1,0:T(8,128)S(1)}, f32[3,27648]{1,0:T(4,128)S(1)}, f32[3,128]{1,0:T(4,128)S(1)}, /*index...) while((s32[]{:T(128)}, f32[8,128]{1,0:T(8,128)S(1)}, ...), condition=%wide.region_7.9_spmd.clone, body=%wide.region_6.8_spmd.clone.sunk | while | flops 13764617 | bytes 82645 | solution.py:64
  (230 shorter events, 55.2 us)
Async XLA Ops:
  3.8 153.8 %all-to-all-start.1 = ((f32[64,3,128]{2,1,0:T(4,128)}), f32[64,3,128]{2,1,0:T(4,128)S(1)}, u32[]{:S(2)}, u32[]{:S(2)}) async-start(f32[64,3,128]{2,1,0:T(4,128)} %broadcast_select_fusion.2), calls=%async_computation.1 | async-start | bytes 262144 | tf_op jit(solution)/shard_map/all_to_all | solution.py:107
  144.5 1.3 copy-start.4
  144.5 1.3 copy-start.5
  145.5 1.1 copy-start
  146.6 22.6 %copy-start.3 = (f32[3,128]{1,0:T(4,128)S(1)}, f32[3,128]{1,0:T(4,128)}, u32[]{:S(2)}) copy-start(f32[3,128]{1,0:T(4,128)} %param.20) | copy-start | bytes 4612
  146.6 22.6 %copy-start.1 = (f32[8,128]{1,0:T(8,128)S(1)}, f32[8,128]{1,0:T(8,128)}, u32[]{:S(2)}) copy-start(f32[8,128]{1,0:T(8,128)} %param.22) | copy-start | bytes 12292
  157.6 31.7 %all-to-all-start = ((f32[64,8,128]{2,1,0:T(8,128)}), f32[64,8,128]{2,1,0:T(8,128)S(1)}, u32[]{:S(2)}, u32[]{:S(2)}) async-start(f32[64,8,128]{2,1,0:T(8,128)} %broadcast_select_fusion.1), calls=%async_computation | async-start | bytes 524288 | tf_op jit(solution)/shard_map/all_to_all | solution.py:118
  205.2 23.9 %copy-start.2 = (f32[8,128]{1,0:T(8,128)S(1)}, f32[8,128]{1,0:T(8,128)}, u32[]{:S(2)}) copy-start(f32[8,128]{1,0:T(8,128)} %param.23) | copy-start | bytes 12292
  205.2 23.9 %copy-start.6 = (f32[8]{0:T(128)S(1)}, f32[8]{0:T(128)}, u32[]{:S(2)}) copy-start(f32[8]{0:T(128)} %param.24) | copy-start | bytes 100
  230.1 138.2 %all-to-all-start.2 = ((f32[64,8,128]{2,1,0:T(8,128)}), f32[64,8,128]{2,1,0:T(8,128)}, u32[]{:S(2)}, u32[]{:S(2)}) async-start(f32[64,8,128]{2,1,0:T(8,128)} %broadcast_select_fusion), calls=%async_computation.2 | async-start | bytes 524288 | tf_op jit(solution)/shard_map/all_to_all | solution.py:118
where the time goes:
time: 409 us; the launch traced here: 408 us
  blocking collectives  279 us (68%)
  matrix products  60.2 us (15%)
  starting transfers between devices  38.4 us (9%)
  local copies, waits for them, and re-layouts  13.7 us (3%)
  other arithmetic  7.24 us (2%)
  waiting for transfers between devices  5.93 us (1%)
    all_gather x2, blocking collectives, body(): lax.all_gather(proxy_charges, ('cluster', 'member'), axis=1, tiled=True)  237 us
    dot_general x58, matrix products, advance(): jnp.dot(wts, kernel, precision=lax.Precision.HIGHEST, preferred_element_t...  60 us
    all_gather x2, blocking collectives, body(): lax.all_gather(near_charges, 'member', axis=0, tiled=True)  28.7 us
    all_to_all x1, starting transfers between devices, body(): lax.all_to_all(outgoing(source_points), 'cluster', split_axis=0, concat_a...  19.3 us
    all_to_all x2, starting transfers between devices, body(): lax.all_to_all(outgoing(current), 'cluster', split_axis=0, concat_axis=0,...  19.1 us
    all_gather x1, blocking collectives, body(): all_near_points = lax.all_gather(near_points, 'member', axis=0, tiled=True)  13.3 us
  transfers between devices with their start and end apart: 3, of which 1 were waited for; matrix products, arithmetic and copies ran while one was open for 7% of the time, Pallas kernels for 0%

commit v1 on v0

--- a/solution.py
+++ b/solution.py
@@ -124,7 +124,8 @@
             flatten_packets(all_near_points),
             flatten_packets(lax.all_gather(near_charges, "member", axis=0, tiled=True)),
         )
-        piece = lax.all_gather(proxy_charges, ("cluster", "member"), axis=1, tiled=True)
+        sent = jnp.stack([proxy_charges] * lax.axis_size(("cluster", "member")))
+        piece = jnp.concatenate(lax.all_to_all(sent, ("cluster", "member"), 0, 0), axis=1)
         positions = lax.slice_in_dim(every_proxy, 0, piece.shape[1], axis=1)
         far_sum = potential(target_points, positions, piece * every_far[None, :])
         field_sum = near_sum + far_sum

time: 409 us -> 249 us (0.61)
  blocking collectives: 279 us -> 51.5 us
  starting transfers between devices: 38.4 us -> 67.6 us
  waiting for transfers between devices: 5.93 us -> 27.9 us
  local copies, waits for them, and re-layouts: 13.7 us -> 24.5 us
  other arithmetic: 7.24 us -> 12.3 us
    all_gather x2 -> x0, blocking collectives: 237 us -> none  [body(): lax.all_gather(proxy_charges, ('cluster', 'member'), axis=1, tiled=True)]
    all_to_all x0 -> x2, starting transfers between devices: none -> 27.4 us  [body(): lax.all_to_all(sent, ('cluster', 'member'), 0, 0)]
    all_to_all x2, waiting for transfers between devices: 5.93 us -> 21.4 us  [body(): lax.all_to_all(outgoing(current), 'cluster', split_axis=0, concat_axis=0,...]
    reshape x0 -> x4, local copies, waits for them, and re-layouts: none -> 8.54 us  [body(): jnp.concatenate(lax.all_to_all(sent, ('cluster', 'member'), 0, 0), axis=1)]
    all_gather x2, blocking collectives: 28.7 us -> 36.7 us  [body(): lax.all_gather(near_charges, 'member', axis=0, tiled=True)]
    all_to_all x1, waiting for transfers between devices: 0.01 us -> 6.48 us  [body(): lax.all_to_all(outgoing(source_points), 'cluster', split_axis=0, concat_a...]
  transfers between devices with their start and end apart: 3 -> 5, of which waited for: 1 -> 3; matrix products, arithmetic and copies ran while one was open for 7% -> 23% of each run, Pallas kernels for 0% -> 0%
where the time goes in v1:
time: 249 us; the launch traced here: 248 us
  starting transfers between devices  67.6 us (27%)
  matrix products  60.2 us (24%)
  blocking collectives  51.5 us (21%)
  waiting for transfers between devices  27.9 us (11%)
  local copies, waits for them, and re-layouts  24.5 us (10%)
  other arithmetic  12.3 us (5%)
    dot_general x58, matrix products, advance(): jnp.dot(wts, kernel, precision=lax.Precision.HIGHEST, preferred_element_t...  60 us
    all_gather x2, blocking collectives, body(): lax.all_gather(near_charges, 'member', axis=0, tiled=True)  36.7 us
    all_to_all x2, starting transfers between devices, body(): lax.all_to_all(sent, ('cluster', 'member'), 0, 0)  27.4 us
    all_to_all x2, waiting for transfers between devices, body(): lax.all_to_all(outgoing(current), 'cluster', split_axis=0, concat_axis=0,...  21.4 us
    all_to_all x2, starting transfers between devices, body(): lax.all_to_all(outgoing(current), 'cluster', split_axis=0, concat_axis=0,...  21 us
    all_to_all x1, starting transfers between devices, body(): lax.all_to_all(outgoing(source_points), 'cluster', split_axis=0, concat_a...  19.3 us
    all_gather x1, blocking collectives, body(): all_near_points = lax.all_gather(near_points, 'member', axis=0, tiled=True)  14.7 us
    reshape x4, local copies, waits for them, and re-layouts, body(): jnp.concatenate(lax.all_to_all(sent, ('cluster', 'member'), 0, 0), axis=1)  8.54 us
  transfers between devices with their start and end apart: 5, of which 3 were waited for; matrix products, arithmetic and copies ran while one was open for 23% of the time, Pallas kernels for 0%

profile of v1, /device:TPU:1, one launch (start us, length us, event | category | flops | bytes accessed | tf_op | source)
XLA Modules:
  0.0 247.7 jit_solution(14835722752383558613)
XLA Ops:
  3.8 19.3 %all-to-all-start.1 = ((f32[64,3,128]{2,1,0:T(4,128)}), f32[64,3,128]{2,1,0:T(4,128)S(1)}, u32[]{:S(2)}, u32[]{:S(2)}) async-start(f32[64,3,128]{2,1,0:T(4,128)} %broadcast_select_fusion.2), calls=%async_computation.1 | async-start | bytes 262144 | tf_op jit(solution)/shard_map/all_to_all | solution.py:107
  30.9 6.5 %all-to-all-done.1 = f32[64,3,128]{2,1,0:T(4,128)S(1)} async-done(((f32[64,3,128]{2,1,0:T(4,128)}), f32[64,3,128]{2,1,0:T(4,128)S(1)}, u32[]{:S(2)}, u32[]{:S(2)}) %all-to-all-start.1) | async-done | bytes 98336 | tf_op jit(solution)/shard_map/all_to_all | solution.py:107
  37.3 8.1 %all-to-all-start = ((f32[64,8,128]{2,1,0:T(8,128)}), f32[64,8,128]{2,1,0:T(8,128)S(1)}, u32[]{:S(2)}, u32[]{:S(2)}) async-start(f32[64,8,128]{2,1,0:T(8,128)} %broadcast_select_fusion.1), calls=%async_computation | async-start | bytes 524288 | tf_op jit(solution)/shard_map/all_to_all | solution.py:118
  46.3 14.7 %all_gather.10 = f32[216,3,128]{2,1,0:T(4,128)S(1)} all-gather(f32[27,3,128]{2,1,0:T(4,128)S(1)} %pad_maximum_fusion.2), channel_id=1, replica_groups=mesh['cluster'=64,'member'=8] {'member'}, dimensions={0}, use_global_device_ids=true | all-gather | bytes 373248 | tf_op jit(solution)/shard_map/all_gather | solution.py:111
  61.0 3.2 %all-to-all-done = f32[64,8,128]{2,1,0:T(8,128)S(1)} async-done(((f32[64,8,128]{2,1,0:T(8,128)}), f32[64,8,128]{2,1,0:T(8,128)S(1)}, u32[]{:S(2)}, u32[]{:S(2)}) %all-to-all-start) | async-done | bytes 262176 | tf_op jit(solution)/shard_map/all_to_all | solution.py:118
  64.2 15.5 %all-to-all-start.2 = ((f32[512,1,256]{2,1,0:T(1,128)}), f32[512,1,256]{2,1,0:T(1,128)S(1)}, u32[]{:S(2)}, u32[]{:S(2)}) async-start(f32[512,1,256]{2,1,0:T(1,128)} %reshape.157), calls=%async_computation.2 | async-start | bytes 1048576 | tf_op jit(solution)/shard_map/all_to_all | solution.py:128
  81.1 18.5 %all_gather.9 = f32[216,8,128]{2,1,0:T(8,128)S(1)} all-gather(f32[27,8,128]{2,1,0:T(8,128)S(1)} %pad_maximum_fusion), channel_id=1, replica_groups=mesh['cluster'=64,'member'=8] {'member'}, dimensions={0}, use_global_device_ids=true | all-gather | bytes 995328 | tf_op jit(solution)/shard_map/all_gather | solution.py:125
  99.7 23.9 %while.56 = (s32[]{:T(128)}, f32[8,128]{1,0:T(8,128)S(1)}, f32[8,27648]{1,0:T(8,128)S(1)}, f32[3,27648]{1,0:T(4,128)S(1)}, f32[3,128]{1,0:T(4,128)S(1)}, /*index...) while((s32[]{:T(128)}, f32[8,128]{1,0:T(8,128)S(1)}, ...), condition=%wide.region_2.4_spmd.clone, body=%wide.region_1.0_spmd.clone.sunk | while | flops 13764617 | bytes 82645 | solution.py:64
  124.8 1.9 reduce.5
  128.8 2.6 %reshape.119 = f32[8,16384]{1,0:T(8,128)S(1)} reshape(f32[8,512,32]{2,1,0:T(8,128)} %copy.14) | data formatting | bytes 1048576 | tf_op jit(solution)/shard_map/reshape | solution.py:128
  131.5 10.0 %while.57 = (s32[]{:T(128)}, f32[8,128]{1,0:T(8,128)S(1)}, f32[8,16384]{1,0:T(8,128)S(1)}, f32[3,16384]{1,0:T(4,128)S(1)}, f32[3,128]{1,0:T(4,128)S(1)}, /*index...) while((s32[]{:T(128)}, f32[8,128]{1,0:T(8,128)S(1)}, ...), condition=%wide.region_5.7_spmd.clone, body=%wide.region_4.6_spmd.clone.sunk | while | flops 110102536 | bytes 570069 | solution.py:64
  131.7 4.8 %fusion.112 = f32[8,128]{1,0:T(8,128)S(1)} fusion(f32[128]{0:T(128)S(1)} %get-tuple-element.677, f32[8192]{0:T(1024)S(1)} %bitcast.105, f32[128]{0:T(128)S(1)} %get-tuple-element.679, f32[8192]{0:T(1024)S(1)} %bitcast.104, f32[128]{0:T(128)S(1)} %get-tuple-element.681, f32[8192]{0:T(1024)S(1)} %bitcast.103, f32[8,16384]{1,0:T(8,128)S(1)} %get-tuple-element.762, ...), kind=kOutput, calls=%fused_computation.46.clone.1 | convolution fusion | flops 110102528 | bytes 370181 | tf_op jit(solution)/shard_map/while/body/eval_jaxpr/dot_general | solution.py:59
  136.7 4.8 %fusion.112 = f32[8,128]{1,0:T(8,128)S(1)} fusion(f32[128]{0:T(128)S(1)} %get-tuple-element.677, f32[8192]{0:T(1024)S(1)} %bitcast.105, f32[128]{0:T(128)S(1)} %get-tuple-element.679, f32[8192]{0:T(1024)S(1)} %bitcast.104, f32[128]{0:T(128)S(1)} %get-tuple-element.681, f32[8192]{0:T(1024)S(1)} %bitcast.103, f32[8,16384]{1,0:T(8,128)S(1)} %get-tuple-element.762, ...), kind=kOutput, calls=%fused_computation.46.clone.1 | convolution fusion | flops 110102528 | bytes 370181 | tf_op jit(solution)/shard_map/while/body/eval_jaxpr/dot_general | solution.py:59
  142.5 12.9 %all-to-all-start.3 = ((f32[64,8,128]{2,1,0:T(8,128)}), f32[64,8,128]{2,1,0:T(8,128)S(1)}, u32[]{:S(2)}, u32[]{:S(2)}) async-start(f32[64,8,128]{2,1,0:T(8,128)} %broadcast_select_fusion), calls=%async_computation.3 | async-start | bytes 524288 | tf_op jit(solution)/shard_map/all_to_all | solution.py:118
  155.7 1.7 reshape.159
  157.4 18.1 %all-to-all-done.3 = f32[64,8,128]{2,1,0:T(8,128)S(1)} async-done(((f32[64,8,128]{2,1,0:T(8,128)}), f32[64,8,128]{2,1,0:T(8,128)S(1)}, u32[]{:S(2)}, u32[]{:S(2)}) %all-to-all-start.3) | async-done | bytes 262176 | tf_op jit(solution)/shard_map/all_to_all | solution.py:118
  175.6 11.9 %all-to-all-start.4 = ((f32[512,1,256]{2,1,0:T(1,128)}), f32[512,1,256]{2,1,0:T(1,128)S(1)}, u32[]{:S(2)}, u32[]{:S(2)}) async-start(f32[512,1,256]{2,1,0:T(1,128)} %reshape.159), calls=%async_computation.4 | async-start | bytes 1048576 | tf_op jit(solution)/shard_map/all_to_all | solution.py:128
  188.3 18.2 %all_gather.11 = f32[216,8,128]{2,1,0:T(8,128)S(1)} all-gather(f32[27,8,128]{2,1,0:T(8,128)S(1)} %pad_maximum_fusion.1), channel_id=1, replica_groups=mesh['cluster'=64,'member'=8] {'member'}, dimensions={0}, use_global_device_ids=true | all-gather | bytes 995328 | tf_op jit(solution)/shard_map/all_gather | solution.py:125
  206.5 23.9 %while.58 = (s32[]{:T(128)}, f32[8,128]{1,0:T(8,128)S(1)}, f32[8,27648]{1,0:T(8,128)S(1)}, f32[3,27648]{1,0:T(4,128)S(1)}, f32[3,128]{1,0:T(4,128)S(1)}, /*index...) while((s32[]{:T(128)}, f32[8,128]{1,0:T(8,128)S(1)}, ...), condition=%wide.region_7.9_spmd.clone, body=%wide.region_6.8_spmd.clone.sunk | while | flops 13764617 | bytes 82645 | solution.py:64
  230.3 1.9 reduce.6
  234.4 2.5 %reshape.123 = f32[8,16384]{1,0:T(8,128)S(1)} reshape(f32[8,512,32]{2,1,0:T(8,128)} %copy.15) | data formatting | bytes 1048576 | tf_op jit(solution)/shard_map/reshape | solution.py:128
  237.0 10.0 %while.59 = (s32[]{:T(128)}, f32[8,128]{1,0:T(8,128)S(1)}, f32[8,16384]{1,0:T(8,128)S(1)}, f32[3,16384]{1,0:T(4,128)S(1)}, f32[3,128]{1,0:T(4,128)S(1)}, /*index...) while((s32[]{:T(128)}, f32[8,128]{1,0:T(8,128)S(1)}, ...), condition=%wide.region_9.11_spmd.clone, body=%wide.region_8.10_spmd.clone.sunk | while | flops 110102536 | bytes 570069 | solution.py:64
  237.3 4.8 %fusion.117 = f32[8,128]{1,0:T(8,128)S(1)} fusion(f32[128]{0:T(128)S(1)} %get-tuple-element.699, f32[8192]{0:T(1024)S(1)} %bitcast.108, f32[128]{0:T(128)S(1)} %get-tuple-element.701, f32[8192]{0:T(1024)S(1)} %bitcast.107, f32[128]{0:T(128)S(1)} %get-tuple-element.703, f32[8192]{0:T(1024)S(1)} %bitcast.106, f32[8,16384]{1,0:T(8,128)S(1)} %get-tuple-element.828, ...), kind=kOutput, calls=%fused_computation.97.clone.1 | convolution fusion | flops 110102528 | bytes 370181 | tf_op jit(solution)/shard_map/while/body/eval_jaxpr/dot_general | solution.py:59
  242.3 4.8 %fusion.117 = f32[8,128]{1,0:T(8,128)S(1)} fusion(f32[128]{0:T(128)S(1)} %get-tuple-element.699, f32[8192]{0:T(1024)S(1)} %bitcast.108, f32[128]{0:T(128)S(1)} %get-tuple-element.701, f32[8192]{0:T(1024)S(1)} %bitcast.107, f32[128]{0:T(128)S(1)} %get-tuple-element.703, f32[8192]{0:T(1024)S(1)} %bitcast.106, f32[8,16384]{1,0:T(8,128)S(1)} %get-tuple-element.828, ...), kind=kOutput, calls=%fused_computation.97.clone.1 | convolution fusion | flops 110102528 | bytes 370181 | tf_op jit(solution)/shard_map/while/body/eval_jaxpr/dot_general | solution.py:59
  (251 shorter events, 67.5 us)
Async XLA Ops:
  3.8 33.6 %all-to-all-start.1 = ((f32[64,3,128]{2,1,0:T(4,128)}), f32[64,3,128]{2,1,0:T(4,128)S(1)}, u32[]{:S(2)}, u32[]{:S(2)}) async-start(f32[64,3,128]{2,1,0:T(4,128)} %broadcast_select_fusion.2), calls=%async_computation.1 | async-start | bytes 262144 | tf_op jit(solution)/shard_map/all_to_all | solution.py:107
  24.0 22.3 %copy-start.5 = (pred[26]{0:T(512)(128)(4,1)}, pred[26]{0:T(512)(128)(4,1)S(1)}, u32[]{:S(2)}) copy-start(pred[26]{0:T(512)(128)(4,1)S(1)} %compare_and_fusion) | copy-start | bytes 82
  27.8 17.7 %copy-start.3 = (f32[3,128]{1,0:T(4,128)S(1)}, f32[3,128]{1,0:T(4,128)}, u32[]{:S(2)}) copy-start(f32[3,128]{1,0:T(4,128)} %param.20) | copy-start | bytes 4612
  27.8 17.8 %copy-start.1 = (f32[8,128]{1,0:T(8,128)S(1)}, f32[8,128]{1,0:T(8,128)}, u32[]{:S(2)}) copy-start(f32[8,128]{1,0:T(8,128)} %param.22) | copy-start | bytes 12292
  30.0 69.7 %copy-start.4 = (s32[1024]{0:T(1024)}, s32[1024]{0:T(1024)S(1)}, u32[]{:S(2)}) copy-start(s32[1024]{0:T(1024)S(1)} %pad_clamp_fusion.1) | copy-start | bytes 12292
  30.0 69.7 %copy-start = (f32[3,128]{1,0:T(4,128)S(1)}, f32[3,128]{1,0:T(4,128)}, u32[]{:S(2)}) copy-start(f32[3,128]{1,0:T(4,128)} %param.21) | copy-start | bytes 4612
  30.0 69.7 %copy-start.8 = (f32[8,128]{1,0:T(8,128)S(1)}, f32[8,128]{1,0:T(8,128)}, u32[]{:S(2)}) copy-start(f32[8,128]{1,0:T(8,128)} %custom-call) | copy-start | bytes 12292
  37.3 26.9 %all-to-all-start = ((f32[64,8,128]{2,1,0:T(8,128)}), f32[64,8,128]{2,1,0:T(8,128)S(1)}, u32[]{:S(2)}, u32[]{:S(2)}) async-start(f32[64,8,128]{2,1,0:T(8,128)} %broadcast_select_fusion.1), calls=%async_computation | async-start | bytes 524288 | tf_op jit(solution)/shard_map/all_to_all | solution.py:118
  64.2 59.4 %all-to-all-start.2 = ((f32[512,1,256]{2,1,0:T(1,128)}), f32[512,1,256]{2,1,0:T(1,128)S(1)}, u32[]{:S(2)}, u32[]{:S(2)}) async-start(f32[512,1,256]{2,1,0:T(1,128)} %reshape.157), calls=%async_computation.2 | async-start | bytes 1048576 | tf_op jit(solution)/shard_map/all_to_all | solution.py:128
  123.6 0.6 copy-start.9
  128.8 2.6 %copy-start.7 = (f32[8,128]{1,0:T(8,128)S(1)}, f32[8,128]{1,0:T(8,128)}, u32[]{:S(2)}) copy-start(f32[8,128]{1,0:T(8,128)} %custom-call.1) | copy-start | bytes 12292
  131.4 10.1 %copy-start.2 = (f32[8,128]{1,0:T(8,128)S(1)}, f32[8,128]{1,0:T(8,128)}, u32[]{:S(2)}) copy-start(f32[8,128]{1,0:T(8,128)} %param.23) | copy-start | bytes 12292
  131.5 10.1 %copy-start.10 = (f32[8,128]{1,0:T(8,128)S(1)}, f32[8,128]{1,0:T(8,128)}, u32[]{:S(2)}) copy-start(f32[8,128]{1,0:T(8,128)} %copy-done.9) | copy-start | bytes 12292
  131.5 10.1 %copy-start.11 = (f32[8]{0:T(128)S(1)}, f32[8]{0:T(128)}, u32[]{:S(2)}) copy-start(f32[8]{0:T(128)} %param.24) | copy-start | bytes 100
  142.5 33.1 %all-to-all-start.3 = ((f32[64,8,128]{2,1,0:T(8,128)}), f32[64,8,128]{2,1,0:T(8,128)S(1)}, u32[]{:S(2)}, u32[]{:S(2)}) async-start(f32[64,8,128]{2,1,0:T(8,128)} %broadcast_select_fusion), calls=%async_computation.3 | async-start | bytes 524288 | tf_op jit(solution)/shard_map/all_to_all | solution.py:118
  155.7 32.4 %copy-start.6 = (pred[26]{0:T(512)(128)(4,1)S(1)}, pred[26]{0:T(512)(128)(4,1)}, u32[]{:S(2)}) copy-start(pred[26]{0:T(512)(128)(4,1)} %copy-done.5) | copy-start | bytes 82
  175.6 54.8 %all-to-all-start.4 = ((f32[512,1,256]{2,1,0:T(1,128)}), f32[512,1,256]{2,1,0:T(1,128)S(1)}, u32[]{:S(2)}, u32[]{:S(2)}) async-start(f32[512,1,256]{2,1,0:T(1,128)} %reshape.159), calls=%async_computation.4 | async-start | bytes 1048576 | tf_op jit(solution)/shard_map/all_to_all | solution.py:128
